TPU v7x, 512 devices: a whole 4x8x8 slice. The times are simulated.
512 devices in a mesh: shard: 128 (over y, z, core), tensor: 4 (over x).
Axes of the slice: x: 4, y: 8, z: 8, core: 2. Of those that a mesh axis runs over, the one named last changes fastest.
Arguments:
- grad_query: bfloat16 [128, 1024, 512], P('shard', None, 'tensor'), may hold values from -8 to 8
- error_query: float32 [128, 1024, 512], P('shard', None, 'tensor'), may hold values from -3 to 3
- grad_output: bfloat16 [128, 512, 1024], P('shard', 'tensor'), may hold values from -8 to 8
- error_output: float32 [128, 512, 1024], P('shard', 'tensor'), may hold values from -3 to 3
- start_query: float32 [512, 32], P('tensor'), may hold values from -6 to 6
- start_output: float32 [1024, 32], replicated, may hold values from -6 to 6
- weight_query: float32 [1024, 512], P('shard', 'tensor'), may hold values from -0.1875 to 0.1875
- weight_output: float32 [512, 1024], P('tensor', 'shard'), may hold values from -0.25 to 0.25
- moment_query: float32 [1024, 512], P('shard', 'tensor'), may hold values from -1.2 to 1.2
- moment_output: float32 [512, 1024], P('tensor', 'shard'), may hold values from -1.2 to 1.2
- grad_vector: bfloat16 [128, 3584], P('shard'), may hold values from -12 to 12
- moment_vector: float32 [3584], P('shard'), may hold values from -1.2 to 1.2
- weight_vector: float32 [3584], P('shard'), may hold values from 0.5 to 1.5
Outputs:
- new_error_query: float32 [128, 1024, 512], P('shard', None, 'tensor')
- new_error_output: float32 [128, 512, 1024], P('shard', 'tensor')
- new_moment_query: float32 [1024, 512], P('shard', 'tensor')
- new_moment_output: float32 [512, 1024], P('tensor', 'shard')
- new_weight_query: float32 [1024, 512], P(None, 'tensor')
- new_weight_output: float32 [512, 1024], P('tensor')
- new_moment_vector: float32 [3584], P('shard')
- new_weight_vector: float32 [3584], replicated
All inputs are finite; a program needn't handle non-finite values.
Results may differ from a plain program's by a relative error of at most 0.0003.
Values sent between devices are 32-bit elements; how exact they have to be, the bound alone decides.
No kernel may reach another device: no remote copies, remote signals or barrier semaphores. Data moves between devices by JAX's collectives and lax.ppermute only.
A program may use at most 64 MiB of HBM per device.

v0:
```python
import jax
import jax.numpy as jnp
from jax import lax
from jax.sharding import PartitionSpec as P

ROUNDS = 2
highest = lax.Precision.HIGHEST


def product(left, right):
    return jnp.dot(left, right, precision=highest, preferred_element_type=jnp.float32)


def product_inner(left, right):
    return lax.dot_general(
        left, right, (((0,), (0,)), ((), ())), precision=highest, preferred_element_type=jnp.float32
    )


def solve_rows(gram, factor):
    lower = jnp.linalg.cholesky(gram)
    return jax.scipy.linalg.solve_triangular(lower, factor.T, lower=True).T


def orthonormal(factor):
    return solve_rows(product_inner(factor, factor), factor)


def orthonormal_rows(factor):
    gram = lax.psum(product_inner(factor, factor), "tensor")
    return solve_rows(gram, factor)


def local(
    grad_query,
    error_query,
    grad_output,
    error_output,
    start_query,
    start_output,
    weight_query,
    weight_output,
    moment_query,
    moment_output,
    grad_vector,
    moment_vector,
    weight_vector,
):
    replicas = lax.axis_size("shard")
    shard_index = lax.axis_index("shard")
    total_query = grad_query[0].astype(jnp.float32) + error_query[0]
    total_output = grad_output[0].astype(jnp.float32) + error_output[0]
    factor_query = start_query
    factor_output = start_output
    for turn in range(ROUNDS):
        part_query = product(total_query, factor_query)
        part_output = product(total_output, factor_output)
        sum_query = lax.psum(part_query, ("shard", "tensor"))
        sum_output = lax.psum(part_output, "shard")
        left_query = orthonormal(sum_query)
        left_output = orthonormal_rows(sum_output)
        right_query_part = product_inner(total_query, left_query)
        right_output_part = product_inner(total_output, left_output)
        factor_query = lax.psum(right_query_part, "shard")
        factor_output = lax.psum(right_output_part, ("shard", "tensor"))
    approx_query = product(left_query, factor_query.T) / replicas
    approx_output = product(left_output, factor_output.T) / replicas
    new_error_query = (total_query - approx_query)[None]
    new_error_output = (total_output - approx_output)[None]
    rows_block = moment_query.shape[0]
    block_query = lax.dynamic_slice_in_dim(approx_query, shard_index * rows_block, rows_block, 0)
    cols_block = moment_output.shape[1]
    block_output = lax.dynamic_slice_in_dim(approx_output, shard_index * cols_block, cols_block, 1)
    new_moment_query = 0.9 * moment_query + block_query
    new_moment_output = 0.9 * moment_output + block_output
    stepped_query = weight_query - 0.01 * new_moment_query
    stepped_output = weight_output - 0.01 * new_moment_output
    local_vector = grad_vector[0].astype(jnp.float32)
    vector_block = moment_vector.shape[0]
    vector_whole = lax.psum(local_vector, "shard")
    vector_part = lax.dynamic_slice_in_dim(
        vector_whole, shard_index * vector_block, vector_block, 0
    )
    vector_mean = vector_part / replicas
    new_moment_vector = 0.9 * moment_vector + vector_mean
    stepped_vector = weight_vector - 0.01 * new_moment_vector
    new_weight_query, new_weight_output, new_weight_vector = (
        lax.all_gather(stepped_query, "shard", axis=0, tiled=True),
        lax.all_gather(stepped_output, "shard", axis=1, tiled=True),
        lax.all_gather(stepped_vector, "shard", axis=0, tiled=True),
    )
    return (
        new_error_query,
        new_error_output,
        new_moment_query,
        new_moment_output,
        new_weight_query,
        new_weight_output,
        new_moment_vector,
        new_weight_vector,
    )


def solution(mesh):
    in_specs = (
        P("shard", None, "tensor"),
        P("shard", None, "tensor"),
        P("shard", "tensor", None),
        P("shard", "tensor", None),
        P("tensor", None),
        P(),
        P("shard", "tensor"),
        P("tensor", "shard"),
        P("shard", "tensor"),
        P("tensor", "shard"),
        P("shard", None),
        P("shard"),
        P("shard"),
    )
    out_specs = (
        P("shard", None, "tensor"),
        P("shard", "tensor", None),
        P("shard", "tensor"),
        P("tensor", "shard"),
        P(None, "tensor"),
        P("tensor", None),
        P("shard"),
        P(),
    )
    return jax.shard_map(local, mesh=mesh, in_specs=in_specs, out_specs=out_specs, check_vma=False)
```

profile of v0, /device:TPU:1, one launch (start us, length us, event | category | flops | bytes accessed | tf_op | source)
XLA Modules:
  0.0 2203.4 jit_solution(7634404734054702130)
XLA Ops:
  9.1 498.1 %psum.81 = f32[128,32]{0,1:T(8,128)S(1)} all-reduce(f32[128,32]{0,1:T(8,128)S(1)} %fusion.6), channel_id=1, replica_groups=mesh['shard'=128,'tensor'=4] {'shard'}, use_global_device_ids=true, to_apply=%region_6.9 | all-reduce | flops 4096 | bytes 32768 | tf_op jit(solution)/shard_map/psum | solution.py:59
  507.3 13.2 psum.82
  520.6 2.9 cholesky.96
  524.9 2.4 custom-call.12
  527.6 1.3 fusion.4
  528.9 1.3 fusion.15
  530.3 1.3 dynamic-slice
  532.3 265.7 %all-reduce.10.cloned.1.call-done = (f32[1024,32]{0,1:T(8,128)}, f32[1024,32]{0,1:T(8,128)}) async-done(((f32[1024,32]{0,1:T(8,128)}, f32[1024,32]{0,1:T(8,128)}), (f32[1024,32]{0,1:T(8,128)}, f32[1024,32]{0,1:T(8,128)})) %all-reduce.10.cloned.1.call-update) | async-done | bytes 262160 | tf_op jit(solution)/shard_map/psum | solution.py:58
  798.0 1.4 fusion.2
  799.7 2.9 cholesky.74
  804.0 2.4 custom-call.10
  807.2 487.8 %all-reduce.4 = (f32[128,32]{0,1:T(8,128)S(1)}, f32[128,32]{0,1:T(8,128)S(1)}, f32[3584]{0:T(1024)S(1)}) all-reduce(f32[128,32]{0,1:T(8,128)S(1)} %fusion.13, f32[128,32]{0,1:T(8,128)S(1)} %fusion.2, f32[3584]{0:T(1024)S(1)} %convert_reduce_fusion), channel_id=1, replica_groups=mesh['shard'=128,'tensor'=4] {'shard'}, use_global_device_ids=true, to_apply=%region_3.6 | all-reduce | flops 11776 | bytes 94208 | tf_op jit(solution)/shard_map/psum | solution.py:64
  1295.2 12.4 psum.85
  1307.6 2.9 cholesky.107
  1311.9 2.4 custom-call.13
  1314.6 1.3 fusion.11
  1315.9 1.3 fusion
  1318.5 270.5 %all-reduce.8.cloned.1.call-done = (f32[1024,32]{0,1:T(8,128)}, f32[1024,32]{0,1:T(8,128)}) async-done(((f32[1024,32]{0,1:T(8,128)}, f32[1024,32]{0,1:T(8,128)}), (f32[1024,32]{0,1:T(8,128)}, f32[1024,32]{0,1:T(8,128)})) %all-reduce.8.cloned.1.call-update) | async-done | bytes 262160 | tf_op jit(solution)/shard_map/psum | solution.py:58
  1589.0 1.2 fusion.41
  1590.3 2.9 cholesky.85
  1594.6 2.4 custom-call.11
  1597.8 487.8 %all-reduce.3 = (f32[128,32]{0,1:T(8,128)S(1)}, f32[3584]{0:T(1024)}) all-reduce(f32[128,32]{0,1:T(8,128)S(1)} %fusion.9, f32[3584]{0:T(1024)S(1)} %get-tuple-element.48), channel_id=1, replica_groups=mesh['shard'=128,'tensor'=4] {'shard'}, use_global_device_ids=true, to_apply=%region_5.8 | all-reduce | flops 7680 | bytes 61440 | tf_op jit(solution)/shard_map/psum | solution.py:64
  2090.2 53.0 %all_gather.10 = f32[128,1024]{0,1:T(8,128)S(1)} all-gather(f32[128,8]{0,1:T(8,128)S(1)} %get-tuple-element.44), channel_id=1, replica_groups=mesh['shard'=128,'tensor'=4] {'shard'}, dimensions={1}, use_global_device_ids=true | all-gather | bytes 528384 | tf_op jit(solution)/shard_map/all_gather | solution.py:89
  2144.9 50.9 %all_gather.9 = f32[1024,128]{1,0:T(8,128)S(1)} all-gather(f32[8,128]{1,0:T(8,128)S(1)} %get-tuple-element.46), channel_id=1, replica_groups=mesh['shard'=128,'tensor'=4] {'shard'}, dimensions={0}, use_global_device_ids=true | all-gather | bytes 528384 | tf_op jit(solution)/shard_map/all_gather | solution.py:88
  (78 shorter events, 18.4 us)
Async XLA Ops:
  7.2 1.5 copy-start
  7.2 1.2 copy-start.5
  7.2 790.8 %all-reduce.10.cloned.1.call-start = ((), (), s32[]{:S(2)}) async-start(), calls=%async_computation.1 | async-start | bytes 524288 | tf_op jit(solution)/shard_map/psum | solution.py:58
  520.6 8.3 copy-start.1
  527.6 1.3 copy-start.2
  527.6 1.3 copy-start.7
  530.3 1058.7 %all-reduce.8.cloned.1.call-start = ((), (), s32[]{:S(2)}) async-start(), calls=%async_computation | async-start | bytes 524288 | tf_op jit(solution)/shard_map/psum | solution.py:58
  530.3 1.9 copy-start.8
  798.0 1.4 copy-start.3
  1317.2 0.7 copy-start.13
  1317.2 0.7 copy-start.14
  1590.2 6.8 copy-start.4
  2086.6 0.9 copy-start.6
  2088.6 1.0 copy-start.9
  2088.6 1.0 copy-start.10
  2143.3 1.0 copy-start.11
  2143.3 1.0 copy-start.12
Sparse Core Ops, SparseCore 0:
  530.4 267.5 all-reduce.9
  1317.3 271.6 all-reduce.7
where the time goes:
time: 2200 us
  blocking collectives  1600 us (73%)
  waiting for transfers between devices  536 us (24%)
  other arithmetic  29.5 us (1%)
    psum x2, blocking collectives, local(): factor_query = lax.psum(right_query_part, 'shard')  976 us
    psum x2, waiting for transfers between devices, local(): sum_query = lax.psum(part_query, ('shard', 'tensor'))  536 us
    psum x1, blocking collectives, local(): sum_output = lax.psum(part_output, 'shard')  498 us
    all_gather x1, blocking collectives, local(): lax.all_gather(stepped_output, 'shard', axis=1, tiled=True)  53 us
    all_gather x1, blocking collectives, local(): lax.all_gather(stepped_query, 'shard', axis=0, tiled=True)  50.9 us
  transfers between devices with their start and end apart: 2, of which 2 were waited for; matrix products, arithmetic and copies ran while one was open for 0% of the time, Pallas kernels for 0%

commit v1 on v0

--- a/solution.py
+++ b/solution.py
@@ -55,7 +55,8 @@
     for turn in range(ROUNDS):
         part_query = product(total_query, factor_query)
         part_output = product(total_output, factor_output)
-        sum_query = lax.psum(part_query, ("shard", "tensor"))
+        partial = lax.psum(part_query, "tensor")
+        sum_query = lax.psum(partial, "shard")
         sum_output = lax.psum(part_output, "shard")
         left_query = orthonormal(sum_query)
         left_output = orthonormal_rows(sum_output)

time: 2200 us -> 2120 us (0.964)
  blocking collectives: 1600 us -> 1100 us
  waiting for transfers between devices: 536 us -> 944 us
    psum x1 -> x0, blocking collectives: 498 us -> none  [local(): sum_output = lax.psum(part_output, 'shard')]
    psum x2 -> x6, waiting for transfers between devices: 536 us -> 944 us  [the longest x2 476 us: local(): factor_output = lax.psum(right_output_part, ('shard', 'tensor'))]
  transfers between devices with their start and end apart: 2 -> 6, of which waited for: 2 -> 6; matrix products, arithmetic and copies ran while one was open for 0% -> 0% of each run, Pallas kernels for 0% -> 0%
where the time goes in v1:
time: 2120 us
  blocking collectives  1100 us (52%)
  waiting for transfers between devices  944 us (45%)
  other arithmetic  29.5 us (1%)
    psum x2, blocking collectives, local(): factor_query = lax.psum(right_query_part, 'shard')  973 us
    psum x2, waiting for transfers between devices, local(): factor_output = lax.psum(right_output_part, ('shard', 'tensor'))  476 us
    psum x2, waiting for transfers between devices, local(): sum_query = lax.psum(partial, 'shard')  367 us
    psum x2, waiting for transfers between devices, local(): partial = lax.psum(part_query, 'tensor')  102 us
    all_gather x1, blocking collectives, local(): lax.all_gather(stepped_query, 'shard', axis=0, tiled=True)  55.5 us
    all_gather x1, blocking collectives, local(): lax.all_gather(stepped_output, 'shard', axis=1, tiled=True)  49 us
  transfers between devices with their start and end apart: 6, of which 6 were waited for; matrix products, arithmetic and copies ran while one was open for 0% of the time, Pallas kernels for 0%

profile of v1, /device:TPU:1, one launch (start us, length us, event | category | flops | bytes accessed | tf_op | source)
XLA Modules:
  0.0 2115.6 jit_solution(723833185253901209)
XLA Ops:
  7.2 2.5 fusion.15
  13.4 52.8 %all-reduce.10.cloned.1.call-done = f32[1024,32]{0,1:T(8,128)} async-done(((f32[1024,32]{0,1:T(8,128)}), f32[1024,32]{0,1:T(8,128)}) %all-reduce.10.cloned.1.call-update) | async-done | bytes 131088 | tf_op jit(solution)/shard_map/psum | solution.py:58
  66.3 188.7 %all-reduce.12.cloned.1.call-done = f32[1024,32]{0,1:T(8,128)} async-done(((f32[1024,32]{0,1:T(8,128)}), f32[1024,32]{0,1:T(8,128)}) %all-reduce.12.cloned.1.call-update) | async-done | bytes 131088 | tf_op jit(solution)/shard_map/psum | solution.py:59
  256.4 2.9 cholesky.74
  260.6 2.4 custom-call.10
  264.8 486.4 %all-reduce.2 = (f32[128,32]{0,1:T(8,128)S(1)}, f32[128,32]{0,1:T(8,128)S(1)}, f32[3584]{0:T(1024)S(1)}) all-reduce(f32[128,32]{0,1:T(8,128)S(1)} %fusion.13, f32[128,32]{0,1:T(8,128)S(1)} %fusion.6, f32[3584]{0:T(1024)S(1)} %convert_reduce_fusion), channel_id=1, replica_groups=mesh['shard'=128,'tensor'=4] {'shard'}, use_global_device_ids=true, to_apply=%region_4.7 | all-reduce | flops 11776 | bytes 94208 | tf_op jit(solution)/shard_map/psum | solution.py:65
  751.3 13.2 psum.98
  764.6 2.9 cholesky.96
  768.8 2.4 custom-call.12
  771.5 1.3 fusion.11
  775.6 48.7 %all-reduce.14.cloned.1.call-done = f32[1024,32]{0,1:T(8,128)} async-done(((f32[1024,32]{0,1:T(8,128)}), f32[1024,32]{0,1:T(8,128)}) %all-reduce.14.cloned.1.call-update) | async-done | bytes 131088 | tf_op jit(solution)/shard_map/psum | solution.py:58
  824.3 269.6 %all-reduce.18.cloned.1.call-done = f32[1024,32]{0,1:T(8,128)} async-done(((f32[1024,32]{0,1:T(8,128)}), f32[1024,32]{0,1:T(8,128)}) %all-reduce.18.cloned.1.call-update) | async-done | bytes 131088 | tf_op jit(solution)/shard_map/psum | solution.py:66
  1094.0 1.3 fusion.2
  1095.3 178.2 %all-reduce.16.cloned.1.call-done = f32[1024,32]{0,1:T(8,128)} async-done(((f32[1024,32]{0,1:T(8,128)}), f32[1024,32]{0,1:T(8,128)}) %all-reduce.16.cloned.1.call-update) | async-done | bytes 131088 | tf_op jit(solution)/shard_map/psum | solution.py:59
  1274.8 2.9 cholesky.85
  1279.1 2.4 custom-call.11
  1282.3 486.4 %all-reduce.1 = (f32[128,32]{0,1:T(8,128)S(1)}, f32[128,32]{0,1:T(8,128)S(1)}, f32[3584]{0:T(1024)}) all-reduce(f32[128,32]{0,1:T(8,128)S(1)} %fusion.9, f32[128,32]{0,1:T(8,128)S(1)} %fusion.2, f32[3584]{0:T(1024)S(1)} %get-tuple-element.45), channel_id=1, replica_groups=mesh['shard'=128,'tensor'=4] {'shard'}, use_global_device_ids=true, to_apply=%region_7.10 | all-reduce | flops 11776 | bytes 94208 | tf_op jit(solution)/shard_map/psum | solution.py:65
  1768.8 13.2 psum.101
  1782.1 2.9 cholesky.107
  1786.4 2.4 custom-call.13
  1792.9 55.5 %all_gather.9 = f32[1024,128]{1,0:T(8,128)S(1)} all-gather(f32[8,128]{1,0:T(8,128)S(1)} %get-tuple-element.43), channel_id=1, replica_groups=mesh['shard'=128,'tensor'=4] {'shard'}, dimensions={0}, use_global_device_ids=true | all-gather | bytes 528384 | tf_op jit(solution)/shard_map/all_gather | solution.py:89
  1848.4 205.9 %all-reduce.20.cloned.1.call-done = f32[1024,32]{0,1:T(8,128)} async-done(((f32[1024,32]{0,1:T(8,128)}), f32[1024,32]{0,1:T(8,128)}) %all-reduce.20.cloned.1.call-update) | async-done | bytes 131088 | tf_op jit(solution)/shard_map/psum | solution.py:66
  2054.3 1.9 convolution_multiply_fusion
  2057.9 49.0 %all_gather.10 = f32[128,1024]{0,1:T(8,128)S(1)} all-gather(f32[128,8]{0,1:T(8,128)S(1)} %get-tuple-element.41), channel_id=1, replica_groups=mesh['shard'=128,'tensor'=4] {'shard'}, dimensions={1}, use_global_device_ids=true | all-gather | bytes 528384 | tf_op jit(solution)/shard_map/all_gather | solution.py:90
  (85 shorter events, 24.3 us)
Async XLA Ops:
  7.2 5.7 copy-start
  7.2 59.0 %all-reduce.10.cloned.1.call-start = ((), (), s32[]{:S(2)}) async-start(), calls=%async_computation | async-start | bytes 262144 | tf_op jit(solution)/shard_map/psum | solution.py:58
  7.2 2.6 copy-start.5
  9.7 1.0 copy-start.4
  9.7 245.3 %all-reduce.12.cloned.1.call-start = ((), (), s32[]{:S(2)}) async-start(), calls=%async_computation.1 | async-start | bytes 262144 | tf_op jit(solution)/shard_map/psum | solution.py:59
  12.9 53.4 %copy-start.6 = (bf16[1,3584]{1,0:T(2,128)(2,1)S(1)}, bf16[1,3584]{1,0:T(2,128)(2,1)}, u32[]{:S(2)}) copy-start(bf16[1,3584]{1,0:T(2,128)(2,1)} %param.28) | copy-start | bytes 21508
  13.3 251.0 %copy-start.1 = (f32[1,1024,128]{2,1,0:T(8,128)S(1)}, f32[1,1024,128]{2,1,0:T(8,128)}, u32[]{:S(2)}) copy-start(f32[1,1024,128]{2,1,0:T(8,128)} %param.19) | copy-start | bytes 1572868
  66.2 758.0 %all-reduce.14.cloned.1.call-start = ((), (), s32[]{:S(2)}) async-start(), calls=%async_computation.2 | async-start | bytes 262144 | tf_op jit(solution)/shard_map/psum | solution.py:58
  256.3 8.0 copy-start.2
  772.8 321.1 %all-reduce.18.cloned.1.call-start = ((), (), s32[]{:S(2)}) async-start(), calls=%async_computation.4 | async-start | bytes 262144 | tf_op jit(solution)/shard_map/psum | solution.py:66
  774.2 499.2 %all-reduce.16.cloned.1.call-start = ((), (), s32[]{:S(2)}) async-start(), calls=%async_computation.3 | async-start | bytes 262144 | tf_op jit(solution)/shard_map/psum | solution.py:59
  774.3 0.7 copy-start.11
  774.3 0.7 copy-start.12
  824.3 1230.0 %all-reduce.20.cloned.1.call-start = ((), (), s32[]{:S(2)}) async-start(), calls=%async_computation.5 | async-start | bytes 262144 | tf_op jit(solution)/shard_map/psum | solution.py:66
  1274.7 6.8 copy-start.3
  1791.4 0.9 copy-start.7
  1791.4 0.9 copy-start.8
  2056.3 1.0 copy-start.9
  2056.3 1.0 copy-start.10
Sparse Core Ops, SparseCore 0:
  10.9 55.2 all-reduce.9
  69.8 185.1 all-reduce.11
  773.0 51.2 all-reduce.13
  829.7 264.2 all-reduce.17
  1097.4 176.0 all-reduce.15
  1790.5 263.7 all-reduce.19

commit v2 on v0

--- a/solution.py
+++ b/solution.py
@@ -5,6 +5,11 @@
 
 ROUNDS = 2
 highest = lax.Precision.HIGHEST
+
+
+def swapped_in(x, axis, d):
+    sent = jnp.stack([x] * lax.axis_size(axis))
+    return jnp.concatenate(lax.all_to_all(sent, axis, 0, 0), axis=d)
 
 
 def product(left, right):
@@ -85,7 +90,7 @@
     new_moment_vector = 0.9 * moment_vector + vector_mean
     stepped_vector = weight_vector - 0.01 * new_moment_vector
     new_weight_query, new_weight_output, new_weight_vector = (
-        lax.all_gather(stepped_query, "shard", axis=0, tiled=True),
+        swapped_in(stepped_query, "shard", 0),
         lax.all_gather(stepped_output, "shard", axis=1, tiled=True),
         lax.all_gather(stepped_vector, "shard", axis=0, tiled=True),
     )

time: 2200 us -> 2170 us (0.986)
  blocking collectives: 1600 us -> 1550 us
    all_gather x1 -> x0, blocking collectives: 50.9 us -> none  [local(): lax.all_gather(stepped_query, 'shard', axis=0, tiled=True)]
  transfers between devices with their start and end apart: 2 -> 3, of which waited for: 2 -> 2; matrix products, arithmetic and copies ran while one was open for 0% -> 0% of each run, Pallas kernels for 0% -> 0%
where the time goes in v2:
time: 2170 us
  blocking collectives  1550 us (71%)
  waiting for transfers between devices  536 us (25%)
  other arithmetic  29.5 us (1%)
    psum x2, blocking collectives, local(): factor_query = lax.psum(right_query_part, 'shard')  976 us
    psum x2, waiting for transfers between devices, local(): sum_query = lax.psum(part_query, ('shard', 'tensor'))  536 us
    psum x1, blocking collectives, local(): sum_output = lax.psum(part_output, 'shard')  498 us
    all_gather x1, blocking collectives, local(): lax.all_gather(stepped_output, 'shard', axis=1, tiled=True)  54.8 us
  transfers between devices with their start and end apart: 3, of which 2 were waited for; matrix products, arithmetic and copies ran while one was open for 0% of the time, Pallas kernels for 0%

profile of v2, /device:TPU:1, one launch (start us, length us, event | category | flops | bytes accessed | tf_op | source)
XLA Modules:
  0.0 2171.5 jit_solution(1115001216945083325)
XLA Ops:
  7.2 1.3 copy.46
  9.2 498.1 %psum.81 = f32[128,32]{0,1:T(8,128)S(1)} all-reduce(f32[128,32]{0,1:T(8,128)S(1)} %fusion.6), channel_id=1, replica_groups=mesh['shard'=128,'tensor'=4] {'shard'}, use_global_device_ids=true, to_apply=%region_6.9 | all-reduce | flops 4096 | bytes 32768 | tf_op jit(solution)/shard_map/psum | solution.py:64
  507.4 13.2 psum.82
  520.7 2.9 cholesky.96
  525.0 2.4 custom-call.12
  527.7 1.3 fusion.4
  529.0 1.3 fusion.15
  530.4 1.3 dynamic-slice
  532.4 265.7 %all-reduce.10.cloned.1.call-done = (f32[1024,32]{0,1:T(8,128)}, f32[1024,32]{0,1:T(8,128)}) async-done(((f32[1024,32]{0,1:T(8,128)}, f32[1024,32]{0,1:T(8,128)}), (f32[1024,32]{0,1:T(8,128)}, f32[1024,32]{0,1:T(8,128)})) %all-reduce.10.cloned.1.call-update) | async-done | bytes 262160 | tf_op jit(solution)/shard_map/psum | solution.py:63
  799.4 2.9 cholesky.74
  803.7 2.4 custom-call.10
  807.8 487.8 %all-reduce.4 = (f32[128,32]{0,1:T(8,128)S(1)}, f32[128,32]{0,1:T(8,128)S(1)}, f32[3584]{0:T(1024)S(1)}) all-reduce(f32[128,32]{0,1:T(8,128)S(1)} %fusion.13, f32[128,32]{0,1:T(8,128)S(1)} %fusion.2, f32[3584]{0:T(1024)S(1)} %convert_reduce_fusion), channel_id=1, replica_groups=mesh['shard'=128,'tensor'=4] {'shard'}, use_global_device_ids=true, to_apply=%region_3.6 | all-reduce | flops 11776 | bytes 94208 | tf_op jit(solution)/shard_map/psum | solution.py:69
  1295.6 1.3 fusion.11
  1297.1 12.3 psum.85
  1309.4 2.9 cholesky.107
  1313.7 2.4 custom-call.13
  1316.4 1.3 fusion
  1319.0 270.6 %all-reduce.8.cloned.1.call-done = (f32[1024,32]{0,1:T(8,128)}, f32[1024,32]{0,1:T(8,128)}) async-done(((f32[1024,32]{0,1:T(8,128)}, f32[1024,32]{0,1:T(8,128)}), (f32[1024,32]{0,1:T(8,128)}, f32[1024,32]{0,1:T(8,128)})) %all-reduce.8.cloned.1.call-update) | async-done | bytes 262160 | tf_op jit(solution)/shard_map/psum | solution.py:63
  1590.9 2.9 cholesky.85
  1595.1 2.4 custom-call.11
  1598.4 487.8 %all-reduce.3 = (f32[128,32]{0,1:T(8,128)S(1)}, f32[3584]{0:T(1024)}) all-reduce(f32[128,32]{0,1:T(8,128)S(1)} %fusion.9, f32[3584]{0:T(1024)S(1)} %get-tuple-element.48), channel_id=1, replica_groups=mesh['shard'=128,'tensor'=4] {'shard'}, use_global_device_ids=true, to_apply=%region_5.8 | all-reduce | flops 7680 | bytes 61440 | tf_op jit(solution)/shard_map/psum | solution.py:69
  2088.6 14.8 all-to-all-start
  2106.1 54.8 %all_gather.6 = f32[128,1024]{0,1:T(8,128)S(1)} all-gather(f32[128,8]{0,1:T(8,128)S(1)} %get-tuple-element.44), channel_id=1, replica_groups=mesh['shard'=128,'tensor'=4] {'shard'}, dimensions={1}, use_global_device_ids=true | all-gather | bytes 528384 | tf_op jit(solution)/shard_map/all_gather | solution.py:94
  2162.8 1.9 copy.63
  (82 shorter events, 20.3 us)
Async XLA Ops:
  7.2 1.6 copy-start
  7.2 1.4 copy-start.5
  7.2 790.9 %all-reduce.10.cloned.1.call-start = ((), (), s32[]{:S(2)}) async-start(), calls=%async_computation.2 | async-start | bytes 524288 | tf_op jit(solution)/shard_map/psum | solution.py:63
  520.7 8.3 copy-start.1
  527.7 1.3 copy-start.2
  527.7 1.3 copy-start.8
  530.3 1059.2 %all-reduce.8.cloned.1.call-start = ((), (), s32[]{:S(2)}) async-start(), calls=%async_computation.1 | async-start | bytes 524288 | tf_op jit(solution)/shard_map/psum | solution.py:63
  530.4 1.9 copy-start.9
  799.3 6.8 copy-start.3
  806.5 0.9 copy-start.6
  1317.7 0.7 copy-start.14
  1317.7 0.7 copy-start.15
  1590.8 6.8 copy-start.4
  2086.2 1.0 copy-start.10
  2086.2 1.0 copy-start.11
  2088.6 14.8 copy-start.7
  2088.6 74.2 %all-to-all-start = ((f32[128,8,128]{2,1,0:T(8,128)}), f32[128,8,128]{2,1,0:T(8,128)}, u32[]{:S(2)}, u32[]{:S(2)}) async-start(f32[128,8,128]{2,1,0:T(8,128)} %stack.2), calls=%async_computation | async-start | bytes 1048576 | tf_op jit(solution)/shard_map/all_to_all | solution.py:12
  2104.5 1.0 copy-start.12
  2104.5 1.0 copy-start.13
Sparse Core Ops, SparseCore 0:
  530.5 267.5 all-reduce.9
  1317.8 271.6 all-reduce.7
